TPU v7x, 32 devices: a whole 2x2x4 slice. The times are simulated.
32 devices in a mesh: tm: 4 (over y, x), space: 8 (over z, core).
Axes of the slice: x: 2, y: 2, z: 4, core: 2. Of those that a mesh axis runs over, the one named last changes fastest.
Arguments:
- vectors: float32 [4, 2, 3, 64, 2048], P('tm', None, None, None, 'space'), may hold values from -6 to 6
- perambulators: float32 [4, 16, 2, 4096], P('tm'), may hold values from -0.75 to 0.75
- shift_steps: int32 [4], P('tm'), may hold values from 1 to 3, as said below
- spin_choice: int32 [4, 3], replicated, may hold values from 0 to 15
Outputs:
- elementals: float32 [4, 64, 2, 4096], P('tm', 'space')
- correlator: float32 [4, 4, 2], P('tm')
Inputs may be any that keep to these rules, and one draw needn't show every extreme that they name: `shift_steps`: every distance from 1 to 3 is taken by at least one source timeslice. `spin_choice`: each entry is alpha 4 + beta for a pair of spin indices.
All inputs are finite; a program needn't handle non-finite values.
Results may differ from a plain program's by a relative error of at most 0.0003.
Values sent between devices are 32-bit elements; how exact they have to be, the bound alone decides.
A program may use at most 64 MiB of HBM per device.

v0:
```python
import math
import jax
import jax.numpy as jnp
from jax import lax
from jax.sharding import PartitionSpec as P

exact_mode = lax.Precision.HIGHEST


def complex_product(left_re, left_im, right_re, right_im):
    return (left_re * right_re - left_im * right_im, left_re * right_im + left_im * right_re)


def rotate(values, places):
    return jnp.concatenate([values[places:], values[:places]], axis=0)


def contract_first(left, right):
    return lax.dot_general(left, right, (((0,), (0,)), ((), ())), precision=exact_mode)


def inner_rows(left, right):
    return lax.dot_general(left, right, (((1,), (1,)), ((), ())), precision=exact_mode)


def complex_einsum(form, left, right):
    first = jnp.einsum(form, left[0], right[0], precision=exact_mode) - jnp.einsum(
        form, left[1], right[1], precision=exact_mode
    )
    second = jnp.einsum(form, left[0], right[1], precision=exact_mode) + jnp.einsum(
        form, left[1], right[0], precision=exact_mode
    )
    return (first, second)


def elemental_rows(vec_re, vec_im, lead_re, lead_im, first_row, row_count, factor):
    sites = vec_re.shape[1]
    nvec = vec_re.shape[2]
    block = math.gcd(row_count, 4)

    def one_block(index):
        offset = first_row + index * block
        part_re = lax.dynamic_slice_in_dim(vec_re, offset, block, 2)[:, :, :, None]
        part_im = lax.dynamic_slice_in_dim(vec_im, offset, block, 2)[:, :, :, None]
        full_re = vec_re[:, :, None, :]
        full_im = vec_im[:, :, None, :]
        one_re, one_im = complex_product(
            rotate(part_re, 1), rotate(part_im, 1), rotate(full_re, 2), rotate(full_im, 2)
        )
        two_re, two_im = complex_product(
            rotate(part_re, 2), rotate(part_im, 2), rotate(full_re, 1), rotate(full_im, 1)
        )
        cross_re = (one_re - two_re).reshape(3 * sites, block * nvec)
        cross_im = (one_im - two_im).reshape(3 * sites, block * nvec)
        out_re = contract_first(lead_re, cross_re) - contract_first(lead_im, cross_im)
        out_im = contract_first(lead_re, cross_im) + contract_first(lead_im, cross_re)
        stacked = jnp.stack([out_re, out_im], 0).reshape(2, nvec, block, nvec)
        return jnp.transpose(stacked, (2, 0, 1, 3)).reshape(block, 2, nvec * nvec) * factor

    result = lax.map(one_block, jnp.arange(row_count // block, dtype=jnp.int32))
    return result.reshape(row_count, 2, nvec * nvec)


def transform_rows(own, mats, nvec):
    combos = mats.shape[0]
    row_count = own.shape[0]
    elem = (own[:, 0].reshape(row_count, nvec, nvec), own[:, 1].reshape(row_count, nvec, nvec))
    first_mat = (
        mats[:, 0, 0].reshape(combos, nvec, nvec),
        mats[:, 0, 1].reshape(combos, nvec, nvec),
    )
    third_mat = (
        mats[:, 2, 0].reshape(combos, nvec, nvec),
        mats[:, 2, 1].reshape(combos, nvec, nvec),
    )
    half = complex_einsum("jik,slk->sjil", elem, third_mat)
    done = complex_einsum("smi,sjil->sjml", first_mat, half)
    return (
        done[0].reshape(combos * row_count, nvec * nvec),
        done[1].reshape(combos * row_count, nvec * nvec),
    )


def pair_sum(sink_rows, trans_re, trans_im, mid_re, mid_im):
    combos = mid_re.shape[0]
    sink_count = sink_rows.shape[0]
    own_count = mid_re.shape[2]
    sink_re = sink_rows[:, 0]
    sink_im = sink_rows[:, 1]
    inner_re = (inner_rows(sink_re, trans_re) + inner_rows(sink_im, trans_im)).reshape(
        sink_count, combos, own_count
    )
    inner_im = (inner_rows(sink_re, trans_im) - inner_rows(sink_im, trans_re)).reshape(
        sink_count, combos, own_count
    )
    total_re = jnp.einsum("srj,rsj->s", mid_re, inner_re, precision=exact_mode) - jnp.einsum(
        "srj,rsj->s", mid_im, inner_im, precision=exact_mode
    )
    total_im = jnp.einsum("srj,rsj->s", mid_re, inner_im, precision=exact_mode) + jnp.einsum(
        "srj,rsj->s", mid_im, inner_re, precision=exact_mode
    )
    return jnp.stack([total_re, total_im], -1)


def shards(vectors, perambulators, shift_steps, spin_choice):
    local_vec = vectors[0]
    nvec = local_vec.shape[2]
    sites = local_vec.shape[3]
    space_count = lax.axis_size("space")
    time_count = lax.axis_size("tm")
    vec_re = jnp.transpose(local_vec[0], (0, 2, 1))
    vec_im = jnp.transpose(local_vec[1], (0, 2, 1))
    lead_re = vec_re.reshape(3 * sites, nvec)
    lead_im = vec_im.reshape(3 * sites, nvec)
    factor = 1.0 / math.sqrt(24.0 * sites * space_count)
    corr_factor = 0.25 / (nvec * math.sqrt(nvec))
    own_count = nvec // space_count
    own_first = lax.axis_index("space") * own_count
    summed = lax.psum(elemental_rows(vec_re, vec_im, lead_re, lead_im, 0, nvec, factor), "space")
    own = lax.dynamic_slice_in_dim(summed, own_first, own_count, 0)
    every_time = lax.all_gather(own[None], "tm", axis=0, tiled=True)
    target = (lax.axis_index("tm") + shift_steps[0]) % time_count
    sink = lax.dynamic_index_in_dim(every_time, target, 0, keepdims=False)
    combos = spin_choice.shape[0]
    spin_pairs = perambulators.shape[1]
    one_hot = (
        spin_choice[:, :, None] == jnp.arange(spin_pairs, dtype=jnp.int32)[None, None, :]
    ).astype(jnp.float32)
    mats = jnp.einsum("sqm,mcf->sqcf", one_hot, perambulators[0], precision=exact_mode)
    trans_re, trans_im = transform_rows(own, mats, nvec)
    mid_re = lax.dynamic_slice_in_dim(
        mats[:, 1, 0].reshape(combos, nvec, nvec), own_first, own_count, 2
    )
    mid_im = lax.dynamic_slice_in_dim(
        mats[:, 1, 1].reshape(combos, nvec, nvec), own_first, own_count, 2
    )
    sink_rows = lax.all_gather(sink, "space", axis=0, tiled=True)
    partial_corr = pair_sum(sink_rows, trans_re, trans_im, mid_re, mid_im)
    correlator = lax.psum(partial_corr, "space") * corr_factor
    return (own[None], correlator[None])


def solution(mesh):
    placed = (P("tm", None, None, None, "space"), P("tm", None, None, None), P("tm"), P())
    return jax.shard_map(
        shards,
        mesh=mesh,
        in_specs=placed,
        out_specs=(P("tm", "space", None, None), P("tm", None, None)),
        check_vma=False,
    )
```

profile of v0, /device:TPU:0, one launch (start us, length us, event | category | flops | bytes accessed | tf_op | source)
XLA Modules:
  0.0 342.0 jit_solution(15728689861665589250)
XLA Ops:
  7.2 1.0 fusion.30
  8.3 1.1 copy_bitcast_fusion
  9.3 1.1 slice_bitcast_fusion.7
  10.5 1.1 slice_bitcast_fusion.11
  11.6 1.1 slice_bitcast_fusion.6
  12.8 1.1 slice_bitcast_fusion.10
  13.9 1.1 copy.20
  15.0 1.1 copy.21
  16.7 163.7 %while.11 = (s32[]{:T(128)}, f32[16,4,2,4096]{3,2,1,0:T(2,128)}, s32[16]{0:T(128)S(1)}, f32[3,256,64]{1,0,2:T(4,128)}, f32[3,256,1,64]{1,0,3,2:T(4,128)S(1)}, /*...) while((s32[]{:T(128)}, f32[16,4,2,4096]{3,2,1,0:T(2,128)}, ...), condition=%wide.region_1.2_spmd, body=%wide.region_0.1_spmd.sunk | while | flops 606842880 | bytes 11387647 | solution.py:60
  21.9 1.4 fusion.77
  32.1 1.4 fusion.77
  42.4 1.4 fusion.77
  52.6 1.4 fusion.77
  62.8 1.4 fusion.77
  73.1 1.4 fusion.77
  83.3 1.4 fusion.77
  93.5 1.4 fusion.77
  103.8 1.4 fusion.77
  114.0 1.4 fusion.77
  124.2 1.4 fusion.77
  134.4 1.4 fusion.77
  144.7 1.4 fusion.77
  154.9 1.4 fusion.77
  165.1 1.4 fusion.77
  175.3 1.4 fusion.77
  180.4 4.1 %copy.22 = f32[64,2,4096]{2,0,1:T(8,128)} copy(f32[64,2,4096]{2,1,0:T(2,128)} %bitcast.264) | data formatting | bytes 4194304 | tf_op jit(solution)/shard_map/reshape | solution.py:61
  184.6 67.9 %all-reduce.2.cloned.1.call-done = f32[64,2,4096]{2,0,1:T(8,128)} async-done(((f32[64,2,4096]{2,0,1:T(8,128)}), f32[64,2,4096]{2,0,1:T(8,128)}) %all-reduce.2.cloned.1.call-update) | async-done | bytes 2097168 | tf_op jit(solution)/shard_map/psum | solution.py:119
  252.5 1.7 constant_dynamic-slice_fusion.3
  255.9 25.2 %all-gather.5.cloned.1.call-done = f32[32,2,4096]{2,0,1:T(8,128)} async-done(((f32[8,2,4096]{2,0,1:T(8,128)}), f32[32,2,4096]{2,0,1:T(8,128)}) %all-gather.5.cloned.1.call-update) | async-done | bytes 1048592 | tf_op jit(solution)/shard_map/all_gather | solution.py:121
  281.1 1.7 constant_dynamic-slice_fusion.2
  283.9 1.0 constant_dynamic-slice_fusion
  285.1 1.0 fusion.20
  286.1 1.0 fusion.24
  287.1 1.0 fusion.5
  288.1 1.0 fusion.16
  289.2 1.0 fusion.6
  290.2 1.0 fusion.3
  291.2 1.3 copy.27
  292.6 1.6 reshape.145
  294.1 1.0 fusion.18
  295.2 1.0 fusion.4
  296.2 1.3 copy.26
  297.5 1.6 reshape.144
  299.1 12.9 %all-gather.7.cloned.1.call-done = f32[1,64,2,4096]{3,1,0,2:T(8,128)} async-done(((f32[1,8,2,4096]{3,1,0,2:T(8,128)}), f32[1,64,2,4096]{3,1,0,2:T(8,128)}) %all-gather.7.cloned.1.call-update) | async-done | bytes 2097168 | tf_op jit(solution)/shard_map/all_gather | solution.py:137
  312.1 2.3 fusion.9
  314.4 2.2 fusion.10
  317.6 1.1 multiply_reduce_fusion.2
  319.6 15.2 %psum.15 = f32[4,2]{0,1:T(2,128)S(1)} all-reduce(f32[4,2]{0,1:T(2,128)S(1)} %pad_maximum_fusion.4), channel_id=1, replica_groups=mesh['tm'=4,'space'=8] {'space'}, use_global_device_ids=true, to_apply=%region_3.4 | all-reduce | flops 8 | bytes 64 | tf_op jit(solution)/shard_map/psum | solution.py:139
  (344 shorter events, 133.5 us)
Async XLA Ops:
  7.2 245.4 %all-reduce.2.cloned.1.call-start = ((), (), s32[]{:S(2)}) async-start(), calls=%async_computation | async-start | bytes 4194304 | tf_op jit(solution)/shard_map/psum | solution.py:119
  184.5 70.6 %copy-start.3 = (s32[4,3]{1,0:T(4,128)S(1)}, s32[4,3]{1,0:T(4,128)}, u32[]{:S(2)}) copy-start(s32[4,3]{1,0:T(4,128)} %param.9) | copy-start | bytes 148
  184.5 70.7 %copy-start.2 = (f32[1,16,2,4096]{3,2,1,0:T(2,128)S(1)}, f32[1,16,2,4096]{3,2,1,0:T(2,128)}, u32[]{:S(2)}) copy-start(f32[1,16,2,4096]{3,2,1,0:T(2,128)} %param.7) | copy-start | bytes 1572868
  184.5 96.6 %all-gather.5.cloned.1.call-start = ((), (), s32[]{:S(2)}) async-start(), calls=%async_computation.1 | async-start | bytes 1310720 | tf_op jit(solution)/shard_map/all_gather | solution.py:121
  254.2 57.9 %all-gather.7.cloned.1.call-start = ((), (), s32[]{:S(2)}) async-start(), calls=%async_computation.2 | async-start | bytes 2359296 | tf_op jit(solution)/shard_map/all_gather | solution.py:137
  312.1 4.5 %copy-start = (f32[1,64,2,4096]{3,1,0,2:T(8,128)S(1)}, f32[1,64,2,4096]{3,1,0,2:T(8,128)}, u32[]{:S(2)}) copy-start(f32[1,64,2,4096]{3,1,0,2:T(8,128)} %all-gather.7.cloned.1.call-done) | copy-start | bytes 6291460
  314.4 4.3 %copy-start.1 = (f32[8,2,4096]{2,0,1:T(8,128)S(1)}, f32[8,2,4096]{2,0,1:T(8,128)}, u32[]{:S(2)}) copy-start(f32[8,2,4096]{2,0,1:T(8,128)} %constant_dynamic-slice_fusion.3) | copy-start | bytes 786436
Sparse Core Ops, SparseCore 0:
  184.6 67.8 all-reduce.1
  254.9 26.0 all-gather.4
  282.9 29.1 all-gather.6
where the time goes:
time: 347 us; the launch traced here: 342 us
  waiting for transfers between devices  106 us (31%)
  local copies, waits for them, and re-layouts  97.5 us (28%)
  matrix products  76.3 us (22%)
  other arithmetic  18.9 us (5%)
  blocking collectives  15.2 us (4%)
  between operations  14.7 us (4%)
  loops' own time  12.9 us (4%)
    psum x1, waiting for transfers between devices, shards(): lax.psum(elemental_rows(vec_re, vec_im, lead_re, lead_im, 0, nvec, factor...  67.9 us
    dot_general x64, matrix products, contract_first(): lax.dot_general(left, right, (((0,), (0,)), ((), ())), precision=exact_mode)  60.9 us
    slice x36, local copies, waits for them, and re-layouts, rotate(): return jnp.concatenate([values[places:], values[:places]], axis=0)  30.9 us
    all_gather x1, waiting for transfers between devices, shards(): every_time = lax.all_gather(own[None], 'tm', axis=0, tiled=True)  25.2 us
    another operation x32, local copies, waits for them, and re-layouts, one_block(): stacked = jnp.stack([out_re, out_im], 0).reshape(2, nvec, block, nvec)  17 us
    sub x16, other arithmetic, one_block(): cross_re = (one_re - two_re).reshape(3 * sites, block * nvec)  15.5 us
    psum x1, blocking collectives, shards(): correlator = lax.psum(partial_corr, 'space') * corr_factor  15.2 us
    all_gather x1, waiting for transfers between devices, shards(): sink_rows = lax.all_gather(sink, 'space', axis=0, tiled=True)  12.9 us
  transfers between devices with their start and end apart: 3, of which 3 were waited for; matrix products, arithmetic and copies ran while one was open for 5% of the time, Pallas kernels for 0%

commit v1 on v0

--- a/solution.py
+++ b/solution.py
@@ -116,7 +116,10 @@
     corr_factor = 0.25 / (nvec * math.sqrt(nvec))
     own_count = nvec // space_count
     own_first = lax.axis_index("space") * own_count
-    summed = lax.psum(elemental_rows(vec_re, vec_im, lead_re, lead_im, 0, nvec, factor), "space")
+    summed = jnp.sum(
+        lax.all_gather(elemental_rows(vec_re, vec_im, lead_re, lead_im, 0, nvec, factor), "space"),
+        axis=0,
+    )
     own = lax.dynamic_slice_in_dim(summed, own_first, own_count, 0)
     every_time = lax.all_gather(own[None], "tm", axis=0, tiled=True)
     target = (lax.axis_index("tm") + shift_steps[0]) % time_count

time: 347 us -> 438 us (1.26)
  waiting for transfers between devices: 106 us -> 190 us
  other arithmetic: 18.9 us -> 26.3 us
    all_gather x0 -> x1, waiting for transfers between devices: none -> 154 us  [shards(): lax.all_gather(elemental_rows(vec_re, vec_im, lead_re, lead_im, 0, nvec,...]
    psum x1 -> x0, waiting for transfers between devices: 67.9 us -> none  [shards(): lax.psum(elemental_rows(vec_re, vec_im, lead_re, lead_im, 0, nvec, factor...]
    reduce_sum x0 -> x1, other arithmetic: none -> 7.37 us  [shards(): jnp.sum(lax.all_gather(elemental_rows(vec_re, vec_im, lead_re, lead_im, 0...]
    slice x0 -> x1, local copies, waits for them, and re-layouts: none -> 4.64 us  [pair_sum(): sink_im = sink_rows[:, 1]]
  transfers between devices with their start and end apart: 3 -> 3, of which waited for: 3 -> 3; matrix products, arithmetic and copies ran while one was open for 5% -> 4% of each run, Pallas kernels for 0% -> 0%
where the time goes in v1:
time: 438 us; the launch traced here: 434 us
  waiting for transfers between devices  190 us (43%)
  local copies, waits for them, and re-layouts  99.8 us (23%)
  matrix products  76.2 us (17%)
  other arithmetic  26.3 us (6%)
  blocking collectives  15.3 us (3%)
  between operations  14.7 us (3%)
  loops' own time  11.8 us (3%)
    all_gather x1, waiting for transfers between devices, shards(): lax.all_gather(elemental_rows(vec_re, vec_im, lead_re, lead_im, 0, nvec,...  154 us
    dot_general x64, matrix products, contract_first(): lax.dot_general(left, right, (((0,), (0,)), ((), ())), precision=exact_mode)  60.9 us
    slice x36, local copies, waits for them, and re-layouts, rotate(): return jnp.concatenate([values[places:], values[:places]], axis=0)  30.9 us
    all_gather x1, waiting for transfers between devices, shards(): every_time = lax.all_gather(own[None], 'tm', axis=0, tiled=True)  23.8 us
    another operation x32, local copies, waits for them, and re-layouts, one_block(): stacked = jnp.stack([out_re, out_im], 0).reshape(2, nvec, block, nvec)  17 us
    sub x16, other arithmetic, one_block(): cross_re = (one_re - two_re).reshape(3 * sites, block * nvec)  15.5 us
    psum x1, blocking collectives, shards(): correlator = lax.psum(partial_corr, 'space') * corr_factor  15.3 us
    all_gather x1, waiting for transfers between devices, shards(): sink_rows = lax.all_gather(sink, 'space', axis=0, tiled=True)  11.9 us
  transfers between devices with their start and end apart: 3, of which 3 were waited for; matrix products, arithmetic and copies ran while one was open for 4% of the time, Pallas kernels for 0%

profile of v1, /device:TPU:0, one launch (start us, length us, event | category | flops | bytes accessed | tf_op | source)
XLA Modules:
  0.0 434.0 jit_solution(424042090725161822)
XLA Ops:
  7.2 1.0 fusion.39
  8.3 1.1 copy_bitcast_fusion
  9.3 1.1 slice_bitcast_fusion.1
  10.5 1.1 slice_bitcast_fusion.5
  11.6 1.1 slice_bitcast_fusion
  12.8 1.1 slice_bitcast_fusion.4
  13.9 1.1 copy.44
  15.0 1.1 copy.45
  16.7 161.5 %while.11 = (s32[]{:T(128)}, f32[16,4,2,4096]{3,2,1,0:T(2,128)}, s32[16]{0:T(128)S(1)}, f32[3,256,64]{1,0,2:T(4,128)}, f32[3,256,1,64]{1,0,3,2:T(4,128)S(1)}, /*...) while((s32[]{:T(128)}, f32[16,4,2,4096]{3,2,1,0:T(2,128)}, ...), condition=%wide.region_1.2_spmd, body=%wide.region_0.1_spmd.sunk | while | flops 606842880 | bytes 11387647 | solution.py:60
  21.8 1.4 fusion.87
  31.9 1.4 fusion.87
  41.9 1.4 fusion.87
  52.0 1.4 fusion.87
  62.1 1.4 fusion.87
  72.2 1.4 fusion.87
  82.3 1.4 fusion.87
  92.4 1.4 fusion.87
  102.5 1.4 fusion.87
  112.6 1.4 fusion.87
  122.7 1.4 fusion.87
  132.8 1.4 fusion.87
  142.9 1.4 fusion.87
  153.0 1.4 fusion.87
  163.0 1.4 fusion.87
  173.2 1.4 fusion.87
  178.2 4.2 copy.82
  182.5 153.9 %all-gather.6.cloned.1.call-done = f32[8,64,2,4096]{3,1,2,0:T(8,128)} async-done(((f32[1,64,2,4096]{3,1,2,0:T(8,128)}), f32[8,64,2,4096]{3,1,2,0:T(8,128)}) %all-gather.6.cloned.1.call-update) | async-done | bytes 16777232 | tf_op jit(solution)/shard_map/all_gather | solution.py:120
  336.4 7.4 %reduce_sum.9 = f32[64,2,4096]{2,0,1:T(8,128)S(1)} reduce(f32[8,64,2,4096]{3,1,2,0:T(8,128)} %all-gather.6.cloned.1.call-done, f32[]{:T(128)} %constant.49.clone.1), dimensions={0}, to_apply=%region_2.3 | reduce | flops 3670016 | bytes 18874372 | tf_op jit(solution)/shard_map/reduce_sum | solution.py:119
  345.7 23.8 %all-gather.8.cloned.1.call-done = f32[32,2,4096]{2,1,0:T(2,128)} async-done(((f32[8,2,4096]{2,1,0:T(2,128)}), f32[32,2,4096]{2,1,0:T(2,128)}) %all-gather.8.cloned.1.call-update) | async-done | bytes 1048592 | tf_op jit(solution)/shard_map/all_gather | solution.py:124
  369.5 1.7 dynamic-slice_bitcast_fusion.8
  374.6 1.0 fusion.28
  376.6 1.0 fusion.5
  377.6 1.0 fusion.24
  378.7 1.0 fusion.6
  379.7 1.0 fusion.3
  380.7 1.3 copy.52
  382.1 1.6 reshape.141
  383.6 1.0 fusion.26
  384.7 1.0 fusion.4
  385.7 1.3 copy.51
  387.1 1.6 reshape.140
  388.6 11.9 %all-gather.10.cloned.1.call-done = f32[1,64,2,4096]{3,2,0,1:T(2,128)} async-done(((f32[1,8,2,4096]{3,2,0,1:T(2,128)}), f32[1,64,2,4096]{3,2,0,1:T(2,128)}) %all-gather.10.cloned.1.call-update) | async-done | bytes 2097168 | tf_op jit(solution)/shard_map/all_gather | solution.py:140
  400.5 4.6 %fusion.37 = (f32[64,1,4096]{2,1,0:T(1,128)S(1)}, f32[64,1,4096]{2,1,0:T(1,128)S(1)}) fusion(f32[64,2,4096]{2,1,0:T(2,128)} %bitcast.260), kind=kLoop, calls=%fused_computation.90 | loop fusion | bytes 4194304 | tf_op jit(solution)/shard_map/slice | solution.py:89
  405.2 1.6 fusion.11
  406.8 1.6 fusion.13
  408.4 1.6 fusion.8
  409.9 1.7 multiply_reduce_fusion.2
  411.7 15.3 %psum.7 = f32[4,2]{0,1:T(2,128)S(1)} all-reduce(f32[4,2]{0,1:T(2,128)S(1)} %pad_maximum_fusion.4), channel_id=1, replica_groups=mesh['tm'=4,'space'=8] {'space'}, use_global_device_ids=true, to_apply=%region_3.4 | all-reduce | flops 8 | bytes 64 | tf_op jit(solution)/shard_map/psum | solution.py:142
  (350 shorter events, 133.8 us)
Async XLA Ops:
  7.2 329.2 %all-gather.6.cloned.1.call-start = ((), (), s32[]{:S(2)}) async-start(), calls=%async_computation | async-start | bytes 18874368 | tf_op jit(solution)/shard_map/all_gather | solution.py:120
  182.4 187.1 %all-gather.8.cloned.1.call-start = ((), (), s32[]{:S(2)}) async-start(), calls=%async_computation.1 | async-start | bytes 1310720 | tf_op jit(solution)/shard_map/all_gather | solution.py:124
  182.5 163.2 %copy-start.5 = (s32[4,3]{1,0:T(4,128)S(1)}, s32[4,3]{1,0:T(4,128)}, u32[]{:S(2)}) copy-start(s32[4,3]{1,0:T(4,128)} %param.9) | copy-start | bytes 148
  343.7 27.5 %copy-start.3 = (f32[1,16,2,4096]{3,2,1,0:T(2,128)S(1)}, f32[1,16,2,4096]{3,2,1,0:T(2,128)}, u32[]{:S(2)}) copy-start(f32[1,16,2,4096]{3,2,1,0:T(2,128)} %param.7) | copy-start | bytes 1572868
  344.7 55.8 %all-gather.10.cloned.1.call-start = ((), (), s32[]{:S(2)}) async-start(), calls=%async_computation.2 | async-start | bytes 2359296 | tf_op jit(solution)/shard_map/all_gather | solution.py:140
  371.2 2.5 copy-start
  372.4 5.2 %copy-start.1 = (f32[4,64,64,1]{2,1,0,3:T(8,128)}, f32[4,64,64,1]{2,1,0,3:T(8,128)S(1)}, u32[]{:S(2)}) copy-start(f32[4,64,64,1]{2,1,0,3:T(8,128)S(1)} %reshape.152) | copy-start | bytes 196612
  380.7 2.9 copy-start.2
  405.2 4.7 %copy-start.4 = (f32[4,8,64]{2,1,0:T(8,128)S(1)}, f32[4,8,64]{2,1,0:T(8,128)}, u32[]{:S(2)}) copy-start(f32[4,8,64]{2,1,0:T(8,128)} %copy.69) | copy-start | bytes 24580
Sparse Core Ops, SparseCore 0:
  182.5 153.7 all-gather.5
  344.8 24.6 all-gather.7
  371.4 29.1 all-gather.9
